TPU v7x, 128 devices: a whole 4x4x4 slice. The times are simulated.
128 devices in a mesh: rows: 8 (over y, core), acts: 16 (over z, x).
Axes of the slice: x: 4, y: 4, z: 4, core: 2. Of those that a mesh axis runs over, the one named last changes fastest.
Arguments:
- features: bfloat16 [32768, 2048], P('rows'), may hold values from -6 to 80
- policy_weight: bfloat16 [2048, 4096], P(None, 'acts'), may hold values from -3 to 3
- reward_weight: bfloat16 [2048, 4096], P(None, 'acts'), may hold values from -1 to 1
- logged_action: int32 [32768], P('rows'), may hold values from 0 to 4095
- reward_level: int32 [32768], P('rows'), may hold values from 0 to 4
- logged_propensity: float32 [32768], P('rows'), may hold values from 9.765625e-05 to 0.0009765625
Outputs:
- policy_grad: float32 [2048, 4096], P(None, 'acts')
- reward_grad: float32 [2048, 4096], P(None, 'acts')
- row_value: float32 [32768], P('rows')
All inputs are finite; a program needn't handle non-finite values.
Results may differ from a plain program's by a relative error of at most 0.015.
Values may be sent and summed in bfloat16 or wider, within the bound.
No kernel may reach another device: no remote copies, remote signals or barrier semaphores. Data moves between devices by JAX's collectives and lax.ppermute only.
A program may use at most 128 MiB of HBM per device.

v0:
```python
import jax
import jax.numpy as jnp
from jax import lax
from jax.sharding import PartitionSpec as P


def finish_rows(
    exponent, row_total, weighted, picked_exp, picked_pred, predicted, onehot, payoff, propensity
):
    probability = exponent / row_total[:, None]
    mean_pred = weighted / row_total
    importance = picked_exp / row_total / propensity
    corrected = importance * (payoff - picked_pred)
    row_value = mean_pred + corrected
    policy_term = (
        probability * (predicted - mean_pred[:, None])
        + corrected[:, None] * (onehot.astype(jnp.float32) - probability)
    ).astype(jnp.bfloat16)
    reward_term = jnp.where(onehot, predicted - payoff[:, None], jnp.float32(0.0)).astype(
        jnp.bfloat16
    )
    return (policy_term, reward_term, row_value)


def on_device(
    features, policy_weight, reward_weight, logged_action, reward_level, logged_propensity
):
    scores = jnp.dot(features, policy_weight, preferred_element_type=jnp.float32)
    predicted = jnp.dot(features, reward_weight, preferred_element_type=jnp.float32)
    act_block = scores.shape[1]
    payoff = reward_level.astype(jnp.float32) * 0.25
    full_scores, full_pred = (
        lax.all_to_all(scores, "acts", split_axis=0, concat_axis=1, tiled=True),
        lax.all_to_all(predicted, "acts", split_axis=0, concat_axis=1, tiled=True),
    )
    part_rows = full_scores.shape[0]
    offset = lax.axis_index("acts") * part_rows
    my_action = lax.dynamic_slice_in_dim(logged_action, offset, part_rows)
    my_payoff = lax.dynamic_slice_in_dim(payoff, offset, part_rows)
    my_propensity = lax.dynamic_slice_in_dim(logged_propensity, offset, part_rows)
    all_columns = jnp.arange(full_scores.shape[1], dtype=jnp.int32)
    row_onehot = my_action[:, None] == all_columns[None, :]
    largest = jnp.max(full_scores, axis=1, keepdims=True)
    exponent = jnp.exp(full_scores - largest)
    row_total = jnp.sum(exponent, axis=1)
    weighted = jnp.sum(exponent * full_pred, axis=1)
    picked_exp = jnp.sum(jnp.where(row_onehot, exponent, jnp.float32(0.0)), axis=1)
    picked_pred = jnp.sum(jnp.where(row_onehot, full_pred, jnp.float32(0.0)), axis=1)
    rows_policy, rows_reward, rows_value = finish_rows(
        exponent,
        row_total,
        weighted,
        picked_exp,
        picked_pred,
        full_pred,
        row_onehot,
        my_payoff,
        my_propensity,
    )
    policy_term, reward_term = (
        lax.all_to_all(rows_policy, "acts", split_axis=1, concat_axis=0, tiled=True),
        lax.all_to_all(rows_reward, "acts", split_axis=1, concat_axis=0, tiled=True),
    )
    row_value = lax.all_gather(rows_value, "acts", axis=0, tiled=True)
    stacked = jnp.concatenate((policy_term, reward_term), axis=1)
    partial_grad = lax.dot_general(
        features, stacked, (((0,), (0,)), ((), ())), preferred_element_type=jnp.float32
    )
    summed = lax.psum(partial_grad.astype(jnp.bfloat16), "rows").astype(jnp.float32)
    return (summed[:, :act_block], summed[:, act_block:], row_value)


def solution(mesh):
    return jax.shard_map(
        on_device,
        mesh=mesh,
        in_specs=(
            P("rows", None),
            P(None, "acts"),
            P(None, "acts"),
            P("rows"),
            P("rows"),
            P("rows"),
        ),
        out_specs=(P(None, "acts"), P(None, "acts"), P("rows")),
        check_vma=False,
    )
```

profile of v0, /device:TPU:0, one launch (start us, length us, event | category | flops | bytes accessed | tf_op | source)
XLA Modules:
  0.0 315.7 jit_solution(8262830132904218718)
XLA Ops:
  7.2 1.2 copy-done
  8.4 10.1 %fusion.24 = f32[4096,256]{1,0:T(8,128)} fusion(bf16[4096,2048]{1,0:T(8,128)(2,1)} %param.6, bf16[2048,256]{1,0:T(8,128)(2,1)S(1)} %copy-done), kind=kOutput, calls=%fused_computation.32 | convolution fusion | flops 4294967296 | bytes 22020096 | tf_op jit(solution)/shard_map/dot_general | solution.py:28
  18.5 8.2 %all-to-all-start = ((f32[16,256,256]{2,1,0:T(8,128)}), f32[16,256,256]{2,1,0:T(8,128)}, u32[]{:S(2)}, u32[]{:S(2)}) async-start(f32[16,256,256]{2,1,0:T(8,128)} %bitcast.37), calls=%async_computation | async-start | bytes 8388608 | tf_op jit(solution)/shard_map/all_to_all | solution.py:33
  26.7 10.1 %fusion.25 = f32[4096,256]{1,0:T(8,128)} fusion(bf16[4096,2048]{1,0:T(8,128)(2,1)} %param.6, bf16[2048,256]{1,0:T(8,128)(2,1)S(1)} %copy-done.1), kind=kOutput, calls=%fused_computation.33 | convolution fusion | flops 4294967296 | bytes 22020096 | tf_op jit(solution)/shard_map/dot_general | solution.py:29
  36.8 53.2 %all-to-all-done = f32[16,256,256]{2,1,0:T(8,128)} async-done(((f32[16,256,256]{2,1,0:T(8,128)}), f32[16,256,256]{2,1,0:T(8,128)}, u32[]{:S(2)}, u32[]{:S(2)}) %all-to-all-start) | async-done | bytes 4194336 | tf_op jit(solution)/shard_map/all_to_all | solution.py:33
  89.9 4.7 %all-to-all-start.1 = ((f32[16,256,256]{2,1,0:T(8,128)}), f32[16,256,256]{2,1,0:T(8,128)}, u32[]{:S(2)}, u32[]{:S(2)}) async-start(f32[16,256,256]{2,1,0:T(8,128)} %bitcast.36), calls=%async_computation.1 | async-start | bytes 8388608 | tf_op jit(solution)/shard_map/all_to_all | solution.py:34
  94.7 0.0 all-reduce.2.cloned.1.call-start
  94.7 0.8 dynamic_slice.9
  95.5 2.5 reduce_max.9
  98.0 2.9 fusion.19
  100.9 54.2 %all-to-all-done.1 = f32[16,256,256]{2,1,0:T(8,128)} async-done(((f32[16,256,256]{2,1,0:T(8,128)}), f32[16,256,256]{2,1,0:T(8,128)}, u32[]{:S(2)}, u32[]{:S(2)}) %all-to-all-start.1) | async-done | bytes 4194336 | tf_op jit(solution)/shard_map/all_to_all | solution.py:34
  155.1 4.5 %fusion.11 = (f32[256]{0:T(256)S(1)}, f32[256]{0:T(256)S(1)}, f32[256]{0:T(256)S(1)}) fusion(f32[16,256,256]{2,1,0:T(8,128)} %all-to-all-done.1, f32[16,256,256]{2,1,0:T(8,128)} %all-to-all-done, f32[256]{0:T(256)S(1)} %reduce_max.9, s32[16,256]{1,0:T(8,128)S(1)} %multiply_add_fusion, s32[256]{0:T(256)S(1)} %dynamic_slice.9), kind=kLoop, calls=%fused_computation.18 | loop fusion | flops 8387840 | bytes 8410112 | tf_op jit(solution)/shard_map/reduce_sum | solution.py:46
  159.6 0.8 fusion.22
  160.4 4.6 %fusion.5 = (bf16[256,16,256]{2,0,1:T(8,128)(2,1)S(1)}, bf16[256,16,256]{2,0,1:T(8,128)(2,1)S(1)}) fusion(f32[16,256,256]{2,1,0:T(8,128)} %all-to-all-done.1, f32[16,256,256]{2,1,0:T(8,128)} %all-to-all-done, f32[256]{0:T(256)S(1)} %get-tuple-element.14, s32[16,256]{1,0:T(8,128)S(1)} %multiply_add_fusion, f32[256]{0:T(256)S(1)} %get-tuple-element.13, ...), kind=kLoop, calls=%fused_computation.9 | loop fusion | flops 13631488 | bytes 12605440 | tf_op jit(solution)/shard_map/convert_element_type | solution.py:18
  165.0 30.2 %all_to_all.61 = bf16[256,16,256]{2,0,1:T(8,128)(2,1)S(1)} all-to-all(bf16[256,16,256]{2,0,1:T(8,128)(2,1)S(1)} %get-tuple-element.15), channel_id=1, replica_groups=mesh['rows'=8,'acts'=16] {'acts'}, dimensions={1} | all-to-all | bytes 4194304 | tf_op jit(solution)/shard_map/all_to_all | solution.py:61
  195.2 28.1 %all_to_all.62 = bf16[256,16,256]{2,0,1:T(8,128)(2,1)S(1)} all-to-all(bf16[256,16,256]{2,0,1:T(8,128)(2,1)S(1)} %get-tuple-element.16), channel_id=1, replica_groups=mesh['rows'=8,'acts'=16] {'acts'}, dimensions={1} | all-to-all | bytes 4194304 | tf_op jit(solution)/shard_map/all_to_all | solution.py:62
  223.2 13.5 %fusion.16 = bf16[2048,512]{0,1:T(8,128)(2,1)} fusion(bf16[4096,2048]{1,0:T(8,128)(2,1)} %param.6, bf16[4096,256]{1,0:T(8,128)(2,1)S(1)} %bitcast.39, bf16[4096,256]{1,0:T(8,128)(2,1)S(1)} %bitcast.38), kind=kOutput, calls=%fused_computation.23 | convolution fusion | flops 8599371776 | bytes 23068672 | tf_op jit(solution)/shard_map/dot_general | solution.py:66
  236.7 0.0 all-reduce.2.cloned.1.call-update
  236.8 21.2 %all-gather = f32[16,1,256]{2,1,0:T(1,128)S(1)} all-gather(f32[1,1,256]{2,1,0:T(1,128)S(1)} %bitcast.41), channel_id=1, replica_groups=mesh['rows'=8,'acts'=16] {'acts'}, dimensions={0}, use_global_device_ids=true | all-gather | bytes 17408 | tf_op jit(solution)/shard_map/all_gather | solution.py:64
  257.9 42.2 %all-reduce.2.cloned.1.call-done = bf16[2048,512]{0,1:T(8,128)(2,1)} async-done(((bf16[2048,512]{0,1:T(8,128)(2,1)}), bf16[2048,512]{0,1:T(8,128)(2,1)}) %all-reduce.2.cloned.1.call-update) | async-done | bytes 2097168 | tf_op jit(solution)/shard_map/psum | solution.py:69
  300.1 3.4 %fusion.23 = (f32[2048,256]{0,1:T(8,128)S(1)}, f32[2048,256]{0,1:T(8,128)}) fusion(bf16[2048,512]{0,1:T(8,128)(2,1)} %all-reduce.2.cloned.1.call-done), kind=kLoop, calls=%fused_computation.31 | loop fusion | bytes 8388608 | tf_op jit(solution)/shard_map/slice | solution.py:70
  303.5 2.9 copy.11
  306.4 1.8 copy.12
  308.2 0.6 copy.15
  (4 shorter events, 0.0 us)
Async XLA Ops:
  7.2 1.2 copy-start
  18.5 8.2 %copy-start.1 = (bf16[2048,256]{1,0:T(8,128)(2,1)S(1)}, bf16[2048,256]{1,0:T(8,128)(2,1)}, u32[]{:S(2)}) copy-start(bf16[2048,256]{1,0:T(8,128)(2,1)} %param.8) | copy-start | bytes 3145732
  18.5 71.5 %all-to-all-start = ((f32[16,256,256]{2,1,0:T(8,128)}), f32[16,256,256]{2,1,0:T(8,128)}, u32[]{:S(2)}, u32[]{:S(2)}) async-start(f32[16,256,256]{2,1,0:T(8,128)} %bitcast.37), calls=%async_computation | async-start | bytes 8388608 | tf_op jit(solution)/shard_map/all_to_all | solution.py:33
  89.9 65.2 %all-to-all-start.1 = ((f32[16,256,256]{2,1,0:T(8,128)}), f32[16,256,256]{2,1,0:T(8,128)}, u32[]{:S(2)}, u32[]{:S(2)}) async-start(f32[16,256,256]{2,1,0:T(8,128)} %bitcast.36), calls=%async_computation.1 | async-start | bytes 8388608 | tf_op jit(solution)/shard_map/all_to_all | solution.py:34
  94.7 205.5 %all-reduce.2.cloned.1.call-start = ((), (), s32[]{:S(2)}) async-start(), calls=%async_computation.4 | async-start | bytes 4194304 | tf_op jit(solution)/shard_map/psum | solution.py:69
Sparse Core Ops, SparseCore 0:
  236.9 63.2 all-reduce.1
where the time goes:
time: 316 us
  waiting for transfers between devices  150 us (47%)
  blocking collectives  79.4 us (25%)
  matrix products  33.7 us (11%)
  other arithmetic  15.2 us (5%)
  between operations  14.1 us (4%)
  starting transfers between devices  12.9 us (4%)
  local copies, waits for them, and re-layouts  10.7 us (3%)
    all_to_all x1, waiting for transfers between devices, on_device(): lax.all_to_all(predicted, 'acts', split_axis=0, concat_axis=1, tiled=True)  54.2 us
    all_to_all x1, waiting for transfers between devices, on_device(): lax.all_to_all(scores, 'acts', split_axis=0, concat_axis=1, tiled=True)  53.2 us
    psum x1, waiting for transfers between devices, on_device(): lax.psum(partial_grad.astype(jnp.bfloat16), 'rows').astype(jnp.float32)  42.2 us
    all_to_all x1, blocking collectives, on_device(): lax.all_to_all(rows_policy, 'acts', split_axis=1, concat_axis=0, tiled=True)  30.2 us
    all_to_all x1, blocking collectives, on_device(): lax.all_to_all(rows_reward, 'acts', split_axis=1, concat_axis=0, tiled=True)  28.1 us
    all_gather x1, blocking collectives, on_device(): row_value = lax.all_gather(rows_value, 'acts', axis=0, tiled=True)  21.2 us
    dot_general x1, matrix products, on_device(): lax.dot_general(features, stacked, (((0,), (0,)), ((), ())), preferred_el...  13.5 us
    dot_general x1, matrix products, on_device(): jnp.dot(features, reward_weight, preferred_element_type=jnp.float32)  10.1 us
  transfers between devices with their start and end apart: 3, of which 3 were waited for; matrix products, arithmetic and copies ran while one was open for 5% of the time, Pallas kernels for 0%

commit v1 on v0

--- a/solution.py
+++ b/solution.py
@@ -61,7 +61,23 @@
         lax.all_to_all(rows_policy, "acts", split_axis=1, concat_axis=0, tiled=True),
         lax.all_to_all(rows_reward, "acts", split_axis=1, concat_axis=0, tiled=True),
     )
-    row_value = lax.all_gather(rows_value, "acts", axis=0, tiled=True)
+    ways, here, step = (lax.axis_size("acts"), lax.axis_index("acts"), rows_value.shape[0])
+    shape = [n * ways if d == 0 else n for d, n in enumerate(rows_value.shape)]
+    full = lax.dynamic_update_slice_in_dim(
+        jnp.zeros(shape, rows_value.dtype), rows_value, here * step, axis=0
+    )
+    going_up = going_down = rows_value
+    for far in range(1, ways // 2 + 1):
+        going_up = lax.ppermute(going_up, "acts", [(d, (d + 1) % ways) for d in range(ways)])
+        full = lax.dynamic_update_slice_in_dim(full, going_up, (here - far) % ways * step, axis=0)
+        if 2 * far < ways:
+            going_down = lax.ppermute(
+                going_down, "acts", [(d, (d - 1) % ways) for d in range(ways)]
+            )
+            full = lax.dynamic_update_slice_in_dim(
+                full, going_down, (here + far) % ways * step, axis=0
+            )
+    row_value = full
     stacked = jnp.concatenate((policy_term, reward_term), axis=1)
     partial_grad = lax.dot_general(
         features, stacked, (((0,), (0,)), ((), ())), preferred_element_type=jnp.float32

time: 316 us -> 317 us (level)
  starting transfers between devices: 12.9 us -> 50.4 us
  blocking collectives: 79.4 us -> 58.8 us
  waiting for transfers between devices: 150 us -> 130 us
    ppermute x0 -> x15, starting transfers between devices: none -> 37.5 us  [the longest x7 36.8 us: on_device(): lax.ppermute(going_down, 'acts', [(d, (d - 1) % ways) for d in range(ways)])]
    psum x1, waiting for transfers between devices: 42.2 us -> 8.25 us  [on_device(): lax.psum(partial_grad.astype(jnp.bfloat16), 'rows').astype(jnp.float32)]
    all_gather x1 -> x0, blocking collectives: 21.2 us -> none  [on_device(): row_value = lax.all_gather(rows_value, 'acts', axis=0, tiled=True)]
    ppermute x0 -> x15, waiting for transfers between devices: none -> 14.4 us  [the longest x8 14.4 us: on_device(): lax.ppermute(going_up, 'acts', [(d, (d + 1) % ways) for d in range(ways)])]
    dynamic_update_slice x0 -> x15, local copies, waits for them, and re-layouts: none -> 3.48 us  [the longest x8 1.78 us: on_device(): lax.dynamic_update_slice_in_dim(full, going_up, (here - far) % ways * ste...]
    unnamed x7 -> x8, local copies, waits for them, and re-layouts: 6.52 us -> 5.92 us
  transfers between devices with their start and end apart: 3 -> 18, of which waited for: 3 -> 11; matrix products, arithmetic and copies ran while one was open for 5% -> 6% of each run, Pallas kernels for 0% -> 0%
where the time goes in v1:
time: 317 us; the launch traced here: 316 us
  waiting for transfers between devices  130 us (41%)
  blocking collectives  58.8 us (19%)
  starting transfers between devices  50.4 us (16%)
  matrix products  33.7 us (11%)
  other arithmetic  15.4 us (5%)
  between operations  14.2 us (4%)
  local copies, waits for them, and re-layouts  13.5 us (4%)
    all_to_all x1, waiting for transfers between devices, on_device(): lax.all_to_all(predicted, 'acts', split_axis=0, concat_axis=1, tiled=True)  54.3 us
    all_to_all x1, waiting for transfers between devices, on_device(): lax.all_to_all(scores, 'acts', split_axis=0, concat_axis=1, tiled=True)  53.2 us
    ppermute x7, starting transfers between devices, on_device(): lax.ppermute(going_down, 'acts', [(d, (d - 1) % ways) for d in range(ways)])  36.8 us
    all_to_all x1, blocking collectives, on_device(): lax.all_to_all(rows_policy, 'acts', split_axis=1, concat_axis=0, tiled=True)  30.2 us
    all_to_all x1, blocking collectives, on_device(): lax.all_to_all(rows_reward, 'acts', split_axis=1, concat_axis=0, tiled=True)  28.6 us
    ppermute x8, waiting for transfers between devices, on_device(): lax.ppermute(going_up, 'acts', [(d, (d + 1) % ways) for d in range(ways)])  14.4 us
    dot_general x1, matrix products, on_device(): lax.dot_general(features, stacked, (((0,), (0,)), ((), ())), preferred_el...  13.5 us
    dot_general x1, matrix products, on_device(): jnp.dot(features, reward_weight, preferred_element_type=jnp.float32)  10.1 us
  transfers between devices with their start and end apart: 18, of which 11 were waited for; matrix products, arithmetic and copies ran while one was open for 6% of the time, Pallas kernels for 0%

profile of v1, /device:TPU:0, one launch (start us, length us, event | category | flops | bytes accessed | tf_op | source)
XLA Modules:
  0.0 316.2 jit_solution(6908113027218442744)
XLA Ops:
  8.4 10.1 %fusion.24 = f32[4096,256]{1,0:T(8,128)} fusion(bf16[4096,2048]{1,0:T(8,128)(2,1)} %param.6, bf16[2048,256]{1,0:T(8,128)(2,1)S(1)} %copy-done), kind=kOutput, calls=%fused_computation.32 | convolution fusion | flops 4294967296 | bytes 22020096 | tf_op jit(solution)/shard_map/dot_general | solution.py:28
  18.5 8.2 %all-to-all-start = ((f32[16,256,256]{2,1,0:T(8,128)}), f32[16,256,256]{2,1,0:T(8,128)}, u32[]{:S(2)}, u32[]{:S(2)}) async-start(f32[16,256,256]{2,1,0:T(8,128)} %bitcast.35), calls=%async_computation | async-start | bytes 8388608 | tf_op jit(solution)/shard_map/all_to_all | solution.py:33
  26.7 10.1 %fusion.25 = f32[4096,256]{1,0:T(8,128)} fusion(bf16[4096,2048]{1,0:T(8,128)(2,1)} %param.6, bf16[2048,256]{1,0:T(8,128)(2,1)S(1)} %copy-done.2), kind=kOutput, calls=%fused_computation.33 | convolution fusion | flops 4294967296 | bytes 22020096 | tf_op jit(solution)/shard_map/dot_general | solution.py:29
  36.8 53.2 %all-to-all-done = f32[16,256,256]{2,1,0:T(8,128)} async-done(((f32[16,256,256]{2,1,0:T(8,128)}), f32[16,256,256]{2,1,0:T(8,128)}, u32[]{:S(2)}, u32[]{:S(2)}) %all-to-all-start) | async-done | bytes 4194336 | tf_op jit(solution)/shard_map/all_to_all | solution.py:33
  89.9 4.7 %all-to-all-start.1 = ((f32[16,256,256]{2,1,0:T(8,128)}), f32[16,256,256]{2,1,0:T(8,128)}, u32[]{:S(2)}, u32[]{:S(2)}) async-start(f32[16,256,256]{2,1,0:T(8,128)} %bitcast.34), calls=%async_computation.1 | async-start | bytes 8388608 | tf_op jit(solution)/shard_map/all_to_all | solution.py:34
  95.5 2.5 reduce_max.9
  98.0 2.9 fusion.19
  100.9 54.3 %all-to-all-done.1 = f32[16,256,256]{2,1,0:T(8,128)} async-done(((f32[16,256,256]{2,1,0:T(8,128)}), f32[16,256,256]{2,1,0:T(8,128)}, u32[]{:S(2)}, u32[]{:S(2)}) %all-to-all-start.1) | async-done | bytes 4194336 | tf_op jit(solution)/shard_map/all_to_all | solution.py:34
  155.1 4.5 %fusion.11 = (f32[256]{0:T(256)S(1)}, f32[256]{0:T(256)S(1)}, f32[256]{0:T(256)S(1)}) fusion(f32[16,256,256]{2,1,0:T(8,128)} %all-to-all-done.1, f32[16,256,256]{2,1,0:T(8,128)} %all-to-all-done, f32[256]{0:T(256)S(1)} %reduce_max.9, s32[16,256]{1,0:T(8,128)S(1)} %multiply_add_fusion, s32[256]{0:T(256)S(1)} %dynamic_slice.9), kind=kLoop, calls=%fused_computation.18 | loop fusion | flops 8387840 | bytes 8410112 | tf_op jit(solution)/shard_map/reduce_sum | solution.py:46
  160.6 4.6 %fusion.5 = (bf16[256,16,256]{2,0,1:T(8,128)(2,1)S(1)}, bf16[256,16,256]{2,0,1:T(8,128)(2,1)S(1)}) fusion(f32[16,256,256]{2,1,0:T(8,128)} %all-to-all-done.1, f32[16,256,256]{2,1,0:T(8,128)} %all-to-all-done, f32[256]{0:T(256)S(1)} %get-tuple-element.12, s32[16,256]{1,0:T(8,128)S(1)} %multiply_add_fusion, f32[256]{0:T(256)S(1)} %get-tuple-element.11, ...), kind=kLoop, calls=%fused_computation.9 | loop fusion | flops 13631488 | bytes 12605440 | tf_op jit(solution)/shard_map/convert_element_type | solution.py:18
  165.1 30.2 %all_to_all.61 = bf16[256,16,256]{2,0,1:T(8,128)(2,1)S(1)} all-to-all(bf16[256,16,256]{2,0,1:T(8,128)(2,1)S(1)} %get-tuple-element.13), channel_id=1, replica_groups=mesh['rows'=8,'acts'=16] {'acts'}, dimensions={1} | all-to-all | bytes 4194304 | tf_op jit(solution)/shard_map/all_to_all | solution.py:61
  195.4 28.6 %all_to_all.62 = bf16[256,16,256]{2,0,1:T(8,128)(2,1)S(1)} all-to-all(bf16[256,16,256]{2,0,1:T(8,128)(2,1)S(1)} %get-tuple-element.14), channel_id=1, replica_groups=mesh['rows'=8,'acts'=16] {'acts'}, dimensions={1} | all-to-all | bytes 4194304 | tf_op jit(solution)/shard_map/all_to_all | solution.py:62
  223.9 13.5 %fusion.16 = bf16[2048,512]{0,1:T(8,128)(2,1)} fusion(bf16[4096,2048]{1,0:T(8,128)(2,1)} %param.6, bf16[4096,256]{1,0:T(8,128)(2,1)S(1)} %bitcast.37, bf16[4096,256]{1,0:T(8,128)(2,1)S(1)} %bitcast.36), kind=kOutput, calls=%fused_computation.23 | convolution fusion | flops 8599371776 | bytes 23068672 | tf_op jit(solution)/shard_map/dot_general | solution.py:82
  238.3 4.7 %collective-permute-start.1 = (f32[256]{0:T(256)S(1)}, f32[256]{0:T(256)S(1)}, u32[]{:S(2)}, u32[]{:S(2)}) collective-permute-start(f32[256]{0:T(256)S(1)} %get-tuple-element.10), channel_id=1, source_target_pairs={{0,15},{1,0},{2,1},{3,2},{4,3},{5,4},{6,5},{7,6},{8,7},{9,8},{10,9... | collective-permute-start | bytes 3080 | tf_op jit(solution)/shard_map/ppermute | solution.py:74
  244.6 5.3 %collective-permute-start.3 = (f32[256]{0:T(256)S(1)}, f32[256]{0:T(256)S(1)}, u32[]{:S(2)}, u32[]{:S(2)}) collective-permute-start(f32[256]{0:T(256)S(1)} %collective-permute-done.1), channel_id=1, source_target_pairs={{0,15},{1,0},{2,1},{3,2},{4,3},{5,4},{6,5},{7,6},{8,7},{9,8},{10,9... | collective-permute-start | bytes 3080 | tf_op jit(solution)/shard_map/ppermute | solution.py:74
  251.5 5.3 %collective-permute-start.5 = (f32[256]{0:T(256)S(1)}, f32[256]{0:T(256)S(1)}, u32[]{:S(2)}, u32[]{:S(2)}) collective-permute-start(f32[256]{0:T(256)S(1)} %collective-permute-done.3), channel_id=1, source_target_pairs={{0,15},{1,0},{2,1},{3,2},{4,3},{5,4},{6,5},{7,6},{8,7},{9,8},{10,9... | collective-permute-start | bytes 3080 | tf_op jit(solution)/shard_map/ppermute | solution.py:74
  258.3 5.3 %collective-permute-start.7 = (f32[256]{0:T(256)S(1)}, f32[256]{0:T(256)S(1)}, u32[]{:S(2)}, u32[]{:S(2)}) collective-permute-start(f32[256]{0:T(256)S(1)} %collective-permute-done.5), channel_id=1, source_target_pairs={{0,15},{1,0},{2,1},{3,2},{4,3},{5,4},{6,5},{7,6},{8,7},{9,8},{10,9... | collective-permute-start | bytes 3080 | tf_op jit(solution)/shard_map/ppermute | solution.py:74
  265.2 5.3 %collective-permute-start.9 = (f32[256]{0:T(256)S(1)}, f32[256]{0:T(256)S(1)}, u32[]{:S(2)}, u32[]{:S(2)}) collective-permute-start(f32[256]{0:T(256)S(1)} %collective-permute-done.7), channel_id=1, source_target_pairs={{0,15},{1,0},{2,1},{3,2},{4,3},{5,4},{6,5},{7,6},{8,7},{9,8},{10,9... | collective-permute-start | bytes 3080 | tf_op jit(solution)/shard_map/ppermute | solution.py:74
  272.1 5.3 %collective-permute-start.11 = (f32[256]{0:T(256)S(1)}, f32[256]{0:T(256)S(1)}, u32[]{:S(2)}, u32[]{:S(2)}) collective-permute-start(f32[256]{0:T(256)S(1)} %collective-permute-done.9), channel_id=1, source_target_pairs={{0,15},{1,0},{2,1},{3,2},{4,3},{5,4},{6,5},{7,6},{8,7},{9,8},{10,9... | collective-permute-start | bytes 3080 | tf_op jit(solution)/shard_map/ppermute | solution.py:74
  279.0 5.3 %collective-permute-start.13 = (f32[256]{0:T(256)S(1)}, f32[256]{0:T(256)S(1)}, u32[]{:S(2)}, u32[]{:S(2)}) collective-permute-start(f32[256]{0:T(256)S(1)} %collective-permute-done.11), channel_id=1, source_target_pairs={{0,15},{1,0},{2,1},{3,2},{4,3},{5,4},{6,5},{7,6},{8,7},{9,8},{10,9... | collective-permute-start | bytes 3080 | tf_op jit(solution)/shard_map/ppermute | solution.py:74
  289.2 3.6 %collective-permute-done.14 = f32[256]{0:T(256)S(1)} collective-permute-done((f32[256]{0:T(256)S(1)}, f32[256]{0:T(256)S(1)}, u32[]{:S(2)}, u32[]{:S(2)}) %collective-permute-start.14) | collective-permute-done | bytes 1056 | tf_op jit(solution)/shard_map/ppermute | solution.py:71
  293.0 8.3 %all-reduce.2.cloned.1.call-done = bf16[2048,512]{0,1:T(8,128)(2,1)} async-done(((bf16[2048,512]{0,1:T(8,128)(2,1)}), bf16[2048,512]{0,1:T(8,128)(2,1)}) %all-reduce.2.cloned.1.call-update) | async-done | bytes 2097168 | tf_op jit(solution)/shard_map/psum | solution.py:85
  301.2 3.4 %fusion.23 = (f32[2048,256]{0,1:T(8,128)}, f32[2048,256]{0,1:T(8,128)S(1)}) fusion(bf16[2048,512]{0,1:T(8,128)(2,1)} %all-reduce.2.cloned.1.call-done), kind=kLoop, calls=%fused_computation.31 | loop fusion | bytes 8388608 | tf_op jit(solution)/shard_map/slice | solution.py:86
  304.6 2.9 copy.10
  (50 shorter events, 19.8 us)
Async XLA Ops:
  7.2 1.2 copy-start
  18.5 8.2 %copy-start.2 = (bf16[2048,256]{1,0:T(8,128)(2,1)S(1)}, bf16[2048,256]{1,0:T(8,128)(2,1)}, u32[]{:S(2)}) copy-start(bf16[2048,256]{1,0:T(8,128)(2,1)} %param.8) | copy-start | bytes 3145732
  18.5 71.5 %all-to-all-start = ((f32[16,256,256]{2,1,0:T(8,128)}), f32[16,256,256]{2,1,0:T(8,128)}, u32[]{:S(2)}, u32[]{:S(2)}) async-start(f32[16,256,256]{2,1,0:T(8,128)} %bitcast.35), calls=%async_computation | async-start | bytes 8388608 | tf_op jit(solution)/shard_map/all_to_all | solution.py:33
  89.9 65.2 %all-to-all-start.1 = ((f32[16,256,256]{2,1,0:T(8,128)}), f32[16,256,256]{2,1,0:T(8,128)}, u32[]{:S(2)}, u32[]{:S(2)}) async-start(f32[16,256,256]{2,1,0:T(8,128)} %bitcast.34), calls=%async_computation.1 | async-start | bytes 8388608 | tf_op jit(solution)/shard_map/all_to_all | solution.py:34
  94.7 206.6 %all-reduce.2.cloned.1.call-start = ((), (), s32[]{:S(2)}) async-start(), calls=%async_computation.4 | async-start | bytes 4194304 | tf_op jit(solution)/shard_map/psum | solution.py:85
  237.6 7.0 %collective-permute-start = (f32[256]{0:T(256)S(1)}, f32[256]{0:T(256)S(1)}, u32[]{:S(2)}, u32[]{:S(2)}) collective-permute-start(f32[256]{0:T(256)S(1)} %get-tuple-element.10), channel_id=1, source_target_pairs={{0,1},{1,2},{2,3},{3,4},{4,5},{5,6},{6,7},{7,8},{8,9},{9,10},{10,1... | collective-permute-start | bytes 3080 | tf_op jit(solution)/shard_map/ppermute | solution.py:71
  238.3 6.3 %collective-permute-start.1 = (f32[256]{0:T(256)S(1)}, f32[256]{0:T(256)S(1)}, u32[]{:S(2)}, u32[]{:S(2)}) collective-permute-start(f32[256]{0:T(256)S(1)} %get-tuple-element.10), channel_id=1, source_target_pairs={{0,15},{1,0},{2,1},{3,2},{4,3},{5,4},{6,5},{7,6},{8,7},{9,8},{10,9... | collective-permute-start | bytes 3080 | tf_op jit(solution)/shard_map/ppermute | solution.py:74
  244.5 6.9 %collective-permute-start.2 = (f32[256]{0:T(256)S(1)}, f32[256]{0:T(256)S(1)}, u32[]{:S(2)}, u32[]{:S(2)}) collective-permute-start(f32[256]{0:T(256)S(1)} %collective-permute-done), channel_id=1, source_target_pairs={{0,1},{1,2},{2,3},{3,4},{4,5},{5,6},{6,7},{7,8},{8,9},{9,10},{10,1... | collective-permute-start | bytes 3080 | tf_op jit(solution)/shard_map/ppermute | solution.py:71
  244.6 6.9 %collective-permute-start.3 = (f32[256]{0:T(256)S(1)}, f32[256]{0:T(256)S(1)}, u32[]{:S(2)}, u32[]{:S(2)}) collective-permute-start(f32[256]{0:T(256)S(1)} %collective-permute-done.1), channel_id=1, source_target_pairs={{0,15},{1,0},{2,1},{3,2},{4,3},{5,4},{6,5},{7,6},{8,7},{9,8},{10,9... | collective-permute-start | bytes 3080 | tf_op jit(solution)/shard_map/ppermute | solution.py:74
  251.4 6.9 %collective-permute-start.4 = (f32[256]{0:T(256)S(1)}, f32[256]{0:T(256)S(1)}, u32[]{:S(2)}, u32[]{:S(2)}) collective-permute-start(f32[256]{0:T(256)S(1)} %collective-permute-done.2), channel_id=1, source_target_pairs={{0,1},{1,2},{2,3},{3,4},{4,5},{5,6},{6,7},{7,8},{8,9},{9,10},{10,1... | collective-permute-start | bytes 3080 | tf_op jit(solution)/shard_map/ppermute | solution.py:71
  251.5 6.9 %collective-permute-start.5 = (f32[256]{0:T(256)S(1)}, f32[256]{0:T(256)S(1)}, u32[]{:S(2)}, u32[]{:S(2)}) collective-permute-start(f32[256]{0:T(256)S(1)} %collective-permute-done.3), channel_id=1, source_target_pairs={{0,15},{1,0},{2,1},{3,2},{4,3},{5,4},{6,5},{7,6},{8,7},{9,8},{10,9... | collective-permute-start | bytes 3080 | tf_op jit(solution)/shard_map/ppermute | solution.py:74
  258.3 6.9 %collective-permute-start.6 = (f32[256]{0:T(256)S(1)}, f32[256]{0:T(256)S(1)}, u32[]{:S(2)}, u32[]{:S(2)}) collective-permute-start(f32[256]{0:T(256)S(1)} %collective-permute-done.4), channel_id=1, source_target_pairs={{0,1},{1,2},{2,3},{3,4},{4,5},{5,6},{6,7},{7,8},{8,9},{9,10},{10,1... | collective-permute-start | bytes 3080 | tf_op jit(solution)/shard_map/ppermute | solution.py:71
  258.3 6.9 %collective-permute-start.7 = (f32[256]{0:T(256)S(1)}, f32[256]{0:T(256)S(1)}, u32[]{:S(2)}, u32[]{:S(2)}) collective-permute-start(f32[256]{0:T(256)S(1)} %collective-permute-done.5), channel_id=1, source_target_pairs={{0,15},{1,0},{2,1},{3,2},{4,3},{5,4},{6,5},{7,6},{8,7},{9,8},{10,9... | collective-permute-start | bytes 3080 | tf_op jit(solution)/shard_map/ppermute | solution.py:74
  265.2 6.9 %collective-permute-start.8 = (f32[256]{0:T(256)S(1)}, f32[256]{0:T(256)S(1)}, u32[]{:S(2)}, u32[]{:S(2)}) collective-permute-start(f32[256]{0:T(256)S(1)} %collective-permute-done.6), channel_id=1, source_target_pairs={{0,1},{1,2},{2,3},{3,4},{4,5},{5,6},{6,7},{7,8},{8,9},{9,10},{10,1... | collective-permute-start | bytes 3080 | tf_op jit(solution)/shard_map/ppermute | solution.py:71
  265.2 6.9 %collective-permute-start.9 = (f32[256]{0:T(256)S(1)}, f32[256]{0:T(256)S(1)}, u32[]{:S(2)}, u32[]{:S(2)}) collective-permute-start(f32[256]{0:T(256)S(1)} %collective-permute-done.7), channel_id=1, source_target_pairs={{0,15},{1,0},{2,1},{3,2},{4,3},{5,4},{6,5},{7,6},{8,7},{9,8},{10,9... | collective-permute-start | bytes 3080 | tf_op jit(solution)/shard_map/ppermute | solution.py:74
  272.1 6.9 %collective-permute-start.10 = (f32[256]{0:T(256)S(1)}, f32[256]{0:T(256)S(1)}, u32[]{:S(2)}, u32[]{:S(2)}) collective-permute-start(f32[256]{0:T(256)S(1)} %collective-permute-done.8), channel_id=1, source_target_pairs={{0,1},{1,2},{2,3},{3,4},{4,5},{5,6},{6,7},{7,8},{8,9},{9,10},{10,1... | collective-permute-start | bytes 3080 | tf_op jit(solution)/shard_map/ppermute | solution.py:71
  272.1 6.9 %collective-permute-start.11 = (f32[256]{0:T(256)S(1)}, f32[256]{0:T(256)S(1)}, u32[]{:S(2)}, u32[]{:S(2)}) collective-permute-start(f32[256]{0:T(256)S(1)} %collective-permute-done.9), channel_id=1, source_target_pairs={{0,15},{1,0},{2,1},{3,2},{4,3},{5,4},{6,5},{7,6},{8,7},{9,8},{10,9... | collective-permute-start | bytes 3080 | tf_op jit(solution)/shard_map/ppermute | solution.py:74
  279.0 6.9 %collective-permute-start.12 = (f32[256]{0:T(256)S(1)}, f32[256]{0:T(256)S(1)}, u32[]{:S(2)}, u32[]{:S(2)}) collective-permute-start(f32[256]{0:T(256)S(1)} %collective-permute-done.10), channel_id=1, source_target_pairs={{0,1},{1,2},{2,3},{3,4},{4,5},{5,6},{6,7},{7,8},{8,9},{9,10},{10,1... | collective-permute-start | bytes 3080 | tf_op jit(solution)/shard_map/ppermute | solution.py:71
  279.0 9.9 %collective-permute-start.13 = (f32[256]{0:T(256)S(1)}, f32[256]{0:T(256)S(1)}, u32[]{:S(2)}, u32[]{:S(2)}) collective-permute-start(f32[256]{0:T(256)S(1)} %collective-permute-done.11), channel_id=1, source_target_pairs={{0,15},{1,0},{2,1},{3,2},{4,3},{5,4},{6,5},{7,6},{8,7},{9,8},{10,9... | collective-permute-start | bytes 3080 | tf_op jit(solution)/shard_map/ppermute | solution.py:74
  285.9 6.9 %collective-permute-start.14 = (f32[256]{0:T(256)S(1)}, f32[256]{0:T(256)S(1)}, u32[]{:S(2)}, u32[]{:S(2)}) collective-permute-start(f32[256]{0:T(256)S(1)} %collective-permute-done.12), channel_id=1, source_target_pairs={{0,1},{1,2},{2,3},{3,4},{4,5},{5,6},{6,7},{7,8},{8,9},{9,10},{10,1... | collective-permute-start | bytes 3080 | tf_op jit(solution)/shard_map/ppermute | solution.py:71
  293.0 11.6 %copy-start.1 = (f32[4096]{0:T(1024)}, f32[4096]{0:T(1024)S(1)}, u32[]{:S(2)}) copy-start(f32[4096]{0:T(1024)S(1)} %dynamic_update_slice.63) | copy-start | bytes 49156
Sparse Core Ops, SparseCore 0:
  237.6 63.6 all-reduce.1
